TPU v7x, 256 devices: a whole 4x4x8 slice. The times are simulated.
256 devices in a mesh: particle: 16 (over z_hi, y), space: 16 (over x, z_lo, core).
Axes of the slice: x: 4, y: 4, z: 8 (z_hi: 4, z_lo: 2; z = z_hi * 2 + z_lo), core: 2. Of those that a mesh axis runs over, the one named last changes fastest.
Arguments:
- ensemble: float32 [16, 13, 512, 1024], P('particle', None, 'space'), may hold values from -6 to 6
- ancestors: int32 [16], replicated, may hold values from 0 to 15
- depth_levels: int32 [512, 1024], P('space'), may hold values from 0 to 4
- level_coefs: float32 [3, 4], replicated, may hold values from 0.25 to 1
- altimetry: float32 [3, 64, 512], P(None, 'particle', 'space'), may hold values from -6 to 6
- obs_rows: int32 [3, 64], replicated, may hold values from 0 to 1023, as said below
Outputs:
- forecast: float32 [16, 13, 512, 1024], P('particle', None, 'space')
Inputs may be any that keep to these rules, and one draw needn't show every extreme that they name: `obs_rows`: within one step the indices are distinct.
All inputs are finite; a program needn't handle non-finite values.
Results may differ from a plain program's by a relative error of at most 0.00013.
Values sent between devices are 32-bit elements; how exact they have to be, the bound alone decides.
A program may use at most 128 MiB of HBM per device.

v0:
```python
import jax
import jax.numpy as jnp
from jax import lax
from jax.sharding import PartitionSpec as P

STEPS = 3
DT = 0.2
CORIOLIS = 0.5
GRAVITY = 1.0
NUDGE = 0.5


def with_halo(block, sides, width):
    for axis, dim in sides:
        count = lax.axis_size(axis)
        forward = [(i, i + 1) for i in range(count - 1)]
        forward.append((count - 1, 0))
        backward = [(target, source) for source, target in forward]
        low = lax.ppermute(
            lax.slice_in_dim(block, block.shape[dim] - width, None, axis=dim), axis, forward
        )
        high = lax.ppermute(lax.slice_in_dim(block, 0, width, axis=dim), axis, backward)
        block = jnp.concatenate([low, block, high], axis=dim)
    return block


def pad_second(field):
    return jnp.pad(field, [(0, 0)] * (field.ndim - 1) + [(1, 1)])


def gradients(wide):
    center = wide[:, 1:-1]
    east = wide[:, 2:]
    west = wide[:, :-2]
    padded = pad_second(center)
    ddx = (east - west) * 0.5
    ddy = (padded[..., 2:] - padded[..., :-2]) * 0.5
    laplace = east + west + padded[..., 2:] + padded[..., :-2] - 4.0 * center
    return (center, ddx, ddy, laplace)


def widen_state(field):
    return with_halo(field, (("space", 1),), 1)


def widen_surface(field):
    return with_halo(field, (("space", 1),), 1)


def level_terms(coefs):
    thick = coefs[0][:, None, None]
    visc = 0.2 * coefs[1][:, None, None]
    kappa = 0.2 * coefs[2][:, None, None]
    return (thick, visc, kappa)


def finish(center, ddx, ddy, laplace, masks, visc, kappa, grad_x, grad_y, height_two):
    levels = masks.shape[0]
    east_vel = center[:levels]
    north_vel = center[levels : 2 * levels]
    temper = center[2 * levels : 3 * levels]
    east_new = masks * (
        east_vel + DT * (CORIOLIS * north_vel - GRAVITY * grad_x + visc * laplace[:levels])
    )
    north_new = masks * (
        north_vel
        + DT * (-CORIOLIS * east_vel - GRAVITY * grad_y + visc * laplace[levels : 2 * levels])
    )
    temper_new = masks * (
        temper
        + DT
        * (
            kappa * laplace[2 * levels : 3 * levels]
            - east_vel * ddx[2 * levels : 3 * levels]
            - north_vel * ddy[2 * levels : 3 * levels]
        )
    )
    return jnp.concatenate([east_new, north_new, temper_new, height_two[None]], axis=0)


def one_step(state, masks, coefs, target, hit):
    levels = masks.shape[0]
    surface = masks[0]
    center, ddx, ddy, laplace = gradients(widen_state(state))
    height = center[3 * levels]
    thick, visc, kappa = level_terms(coefs)
    spread = ddx[:levels] + ddy[levels : 2 * levels]
    height_one = surface * (height - DT * jnp.sum(thick * masks * spread, axis=0))
    height_two = surface * (height_one + NUDGE * hit * (target - height_one))
    unused, grad_x, grad_y, unused_lap = gradients(widen_surface(height_two[None]))
    return finish(center, ddx, ddy, laplace, masks, visc, kappa, grad_x, grad_y, height_two)


def per_device(ensemble, ancestors, depth_levels, level_coefs, altimetry, obs_rows):
    levels = level_coefs.shape[1]
    width_y = ensemble.shape[3]
    mine = ancestors[lax.axis_index("particle")]
    piece = lax.all_gather(ensemble, "particle", axis=0, tiled=True)
    count = piece.shape[0]
    inside = (mine >= 0) & (mine < count)
    chosen = lax.dynamic_index_in_dim(piece, jnp.clip(mine, 0, count - 1), 0, keepdims=False)
    state = jnp.where(inside, chosen, jnp.zeros(ensemble.shape[1:], jnp.float32))
    level_ids = jnp.arange(levels, dtype=jnp.int32)
    masks = (level_ids[:, None, None] < depth_levels[None]).astype(jnp.float32)
    full_mask = jnp.concatenate([masks, masks, masks, masks[:1]], axis=0)
    state = state * full_mask
    columns = jnp.arange(width_y, dtype=jnp.int32)
    for step in range(STEPS):
        lines = lax.all_gather(altimetry[step], "particle", axis=0, tiled=True)
        onehot = (obs_rows[step][:, None] == columns[None, :]).astype(jnp.float32)
        target = jnp.dot(
            lines.T, onehot, precision=lax.Precision.HIGHEST, preferred_element_type=jnp.float32
        )
        hit = jnp.sum(onehot, axis=0)[None, :]
        state = one_step(state, masks, level_coefs, target, hit)
    return state[None]


def solution(mesh):
    in_specs = (
        P("particle", None, "space", None),
        P(),
        P("space", None),
        P(),
        P(None, "particle", "space"),
        P(),
    )
    out_specs = P("particle", None, "space", None)
    return jax.shard_map(
        per_device, mesh=mesh, in_specs=in_specs, out_specs=out_specs, check_vma=False
    )
```

profile of v0, /device:TPU:8, one launch (start us, length us, event | category | flops | bytes accessed | tf_op | source)
XLA Modules:
  0.0 483.3 jit_solution(3686461918665860004)
XLA Ops:
  6.6 0.7 all-gather.5.cloned.1.call-update
  7.3 0.6 dynamic_slice.7
  9.9 0.1 convert_reduce_fusion.2
  10.1 312.0 %all-gather.5.cloned.1.call-done = f32[16,13,32,1024]{3,2,1,0:T(8,128)} async-done(((f32[1,13,32,1024]{3,2,1,0:T(8,128)}), f32[16,13,32,1024]{3,2,1,0:T(8,128)}) %all-gather.5.cloned.1.call-update) | async-done | bytes 27262992 | tf_op jit(solution)/shard_map/all_gather | solution.py:98
  322.1 1.7 maximum_multiply_fusion
  323.9 0.1 collective-permute-start
  324.0 0.5 collective-permute-start.1
  324.5 40.4 %all-gather = f32[1,64,32]{2,0,1:T(1,128)S(1)} all-gather(f32[1,4,32]{2,0,1:T(1,128)S(1)} %bitcast.108), channel_id=2, replica_groups=mesh['particle'=16,'space'=16] {'particle'}, dimensions={1}, use_global_device_ids=true | all-gather | bytes 8704 | tf_op jit(solution)/shard_map/all_gather | solution.py:109
  364.9 1.8 multiply_subtract_fusion.2
  366.7 0.2 fusion.13
  366.9 0.3 fusion.3
  367.2 0.1 collective-permute-start.2
  367.3 0.5 collective-permute-start.3
  367.8 0.1 convert_reduce_fusion.1
  367.9 0.7 collective-permute-done.2
  368.6 3.9 collective-permute-done.3
  372.5 0.1 fusion.73
  372.6 0.6 fusion.54
  373.3 0.2 pad_maximum_fusion.18
  373.5 0.1 collective-permute-start.4
  373.6 0.5 collective-permute-start.5
  374.1 43.4 %all-gather.1 = f32[1,64,32]{2,0,1:T(1,128)S(1)} all-gather(f32[1,4,32]{2,0,1:T(1,128)S(1)} %bitcast.107), channel_id=3, replica_groups=mesh['particle'=16,'space'=16] {'particle'}, dimensions={1}, use_global_device_ids=true | all-gather | bytes 8704 | tf_op jit(solution)/shard_map/all_gather | solution.py:109
  417.5 0.4 subtract_multiply_fusion.3
  417.9 2.1 multiply_subtract_fusion.1
  420.0 0.5 fusion.32
  420.6 0.3 fusion.7
  420.9 0.1 collective-permute-start.6
  421.0 0.5 collective-permute-start.7
  421.5 0.1 convert_reduce_fusion
  421.6 0.7 collective-permute-done.6
  422.3 4.1 collective-permute-done.7
  426.4 0.1 fusion.70
  426.5 0.4 fusion.41
  426.9 0.2 pad_maximum_fusion.19
  427.2 0.1 collective-permute-start.8
  427.3 0.5 collective-permute-start.9
  427.8 38.1 %all-gather.2 = f32[1,64,32]{2,0,1:T(1,128)S(1)} all-gather(f32[1,4,32]{2,0,1:T(1,128)S(1)} %bitcast.106), channel_id=4, replica_groups=mesh['particle'=16,'space'=16] {'particle'}, dimensions={1}, use_global_device_ids=true | all-gather | bytes 8704 | tf_op jit(solution)/shard_map/all_gather | solution.py:109
  465.9 0.4 subtract_multiply_fusion.1
  466.4 2.1 multiply_subtract_fusion
  468.4 0.5 fusion.19
  469.0 0.3 fusion.12
  469.3 0.1 collective-permute-start.10
  469.4 0.5 collective-permute-start.11
  469.9 0.8 collective-permute-done.10
  470.7 3.9 collective-permute-done.11
  474.6 0.1 fusion.67
  474.7 0.4 fusion.28
  475.1 1.3 maximum_bitcast_fusion
  (31 shorter events, 0.4 us)
Async XLA Ops:
  6.5 0.7 copy-start.4
  6.5 3.3 copy-start
  6.5 3.4 copy-start.2
  6.5 3.5 copy-start.1
  6.5 315.6 %all-gather.5.cloned.1.call-start = ((), (), s32[]{:S(2)}) async-start(), calls=%async_computation | async-start | bytes 28966912 | tf_op jit(solution)/shard_map/all_gather | solution.py:98
  322.1 2.4 copy-start.3
  323.9 41.0 %collective-permute-start = (f32[13,1,1024]{2,1,0:T(1,128)S(1)}, f32[13,1,1024]{2,1,0:T(1,128)S(1)}, u32[]{:S(2)}, u32[]{:S(2)}) collective-permute-start(f32[13,1,1024]{2,1,0:T(1,128)S(1)} %get-tuple-element.28), channel_id=1, source_target_pairs={{1,0},{2,1},{3,2},{4,3},{5,4},{6,5},{7,6},{8,7},{9,8},{10,9},{11,1... | collective-permute-start | bytes 159752 | tf_op jit(solution)/shard_map/ppermute | solution.py:22
  324.0 40.9 %collective-permute-start.1 = (f32[13,1,1024]{2,1,0:T(1,128)S(1)}, f32[13,1,1024]{2,1,0:T(1,128)S(1)}, u32[]{:S(2)}, u32[]{:S(2)}) collective-permute-start(f32[13,1,1024]{2,1,0:T(1,128)S(1)} %get-tuple-element.27), channel_id=1, source_target_pairs={{0,1},{1,2},{2,3},{3,4},{4,5},{5,6},{6,7},{7,8},{8,9},{9,10},{10,1... | collective-permute-start | bytes 159752 | tf_op jit(solution)/shard_map/ppermute | solution.py:19
  367.2 1.4 collective-permute-start.2
  367.3 5.2 %collective-permute-start.3 = (f32[1,1,1024]{2,1,0:T(1,128)S(1)}, f32[1,1,1024]{2,1,0:T(1,128)S(1)}, u32[]{:S(2)}, u32[]{:S(2)}) collective-permute-start(f32[1,1,1024]{2,1,0:T(1,128)S(1)} %get-tuple-element.40), channel_id=1, source_target_pairs={{0,1},{1,2},{2,3},{3,4},{4,5},{5,6},{6,7},{7,8},{8,9},{9,10},{10,1... | collective-permute-start | bytes 12296 | tf_op jit(solution)/shard_map/ppermute | solution.py:19
  373.5 43.9 %collective-permute-start.4 = (f32[13,1,1024]{2,1,0:T(1,128)S(1)}, f32[13,1,1024]{2,1,0:T(1,128)S(1)}, u32[]{:S(2)}, u32[]{:S(2)}) collective-permute-start(f32[13,1,1024]{2,1,0:T(1,128)S(1)} %get-tuple-element.25), channel_id=1, source_target_pairs={{1,0},{2,1},{3,2},{4,3},{5,4},{6,5},{7,6},{8,7},{9,8},{10,9},{11,1... | collective-permute-start | bytes 159752 | tf_op jit(solution)/shard_map/ppermute | solution.py:22
  373.6 43.9 %collective-permute-start.5 = (f32[13,1,1024]{2,1,0:T(1,128)S(1)}, f32[13,1,1024]{2,1,0:T(1,128)S(1)}, u32[]{:S(2)}, u32[]{:S(2)}) collective-permute-start(f32[13,1,1024]{2,1,0:T(1,128)S(1)} %get-tuple-element.24), channel_id=1, source_target_pairs={{0,1},{1,2},{2,3},{3,4},{4,5},{5,6},{6,7},{7,8},{8,9},{9,10},{10,1... | collective-permute-start | bytes 159752 | tf_op jit(solution)/shard_map/ppermute | solution.py:19
  420.9 1.4 collective-permute-start.6
  421.0 5.4 %collective-permute-start.7 = (f32[1,1,1024]{2,1,0:T(1,128)S(1)}, f32[1,1,1024]{2,1,0:T(1,128)S(1)}, u32[]{:S(2)}, u32[]{:S(2)}) collective-permute-start(f32[1,1,1024]{2,1,0:T(1,128)S(1)} %get-tuple-element.36), channel_id=1, source_target_pairs={{0,1},{1,2},{2,3},{3,4},{4,5},{5,6},{6,7},{7,8},{8,9},{9,10},{10,1... | collective-permute-start | bytes 12296 | tf_op jit(solution)/shard_map/ppermute | solution.py:19
  427.2 38.7 %collective-permute-start.8 = (f32[13,1,1024]{2,1,0:T(1,128)S(1)}, f32[13,1,1024]{2,1,0:T(1,128)S(1)}, u32[]{:S(2)}, u32[]{:S(2)}) collective-permute-start(f32[13,1,1024]{2,1,0:T(1,128)S(1)} %get-tuple-element.21), channel_id=1, source_target_pairs={{1,0},{2,1},{3,2},{4,3},{5,4},{6,5},{7,6},{8,7},{9,8},{10,9},{11,1... | collective-permute-start | bytes 159752 | tf_op jit(solution)/shard_map/ppermute | solution.py:22
  427.3 38.6 %collective-permute-start.9 = (f32[13,1,1024]{2,1,0:T(1,128)S(1)}, f32[13,1,1024]{2,1,0:T(1,128)S(1)}, u32[]{:S(2)}, u32[]{:S(2)}) collective-permute-start(f32[13,1,1024]{2,1,0:T(1,128)S(1)} %get-tuple-element.20), channel_id=1, source_target_pairs={{0,1},{1,2},{2,3},{3,4},{4,5},{5,6},{6,7},{7,8},{8,9},{9,10},{10,1... | collective-permute-start | bytes 159752 | tf_op jit(solution)/shard_map/ppermute | solution.py:19
  469.3 1.4 collective-permute-start.10
  469.4 5.2 %collective-permute-start.11 = (f32[1,1,1024]{2,1,0:T(1,128)S(1)}, f32[1,1,1024]{2,1,0:T(1,128)S(1)}, u32[]{:S(2)}, u32[]{:S(2)}) collective-permute-start(f32[1,1,1024]{2,1,0:T(1,128)S(1)} %get-tuple-element.32), channel_id=1, source_target_pairs={{0,1},{1,2},{2,3},{3,4},{4,5},{5,6},{6,7},{7,8},{8,9},{9,10},{10,1... | collective-permute-start | bytes 12296 | tf_op jit(solution)/shard_map/ppermute | solution.py:19
Sparse Core Ops, SparseCore 0:
  9.8 312.2 all-gather.4
where the time goes:
time: 483 us
  waiting for transfers between devices  327 us (68%)
  blocking collectives  122 us (25%)
  between operations  15.7 us (3%)
  other arithmetic  13.6 us (3%)
    all_gather x1, waiting for transfers between devices, per_device(): piece = lax.all_gather(ensemble, 'particle', axis=0, tiled=True)  312 us
    all_gather x3, blocking collectives, per_device(): lines = lax.all_gather(altimetry[step], 'particle', axis=0, tiled=True)  122 us
    ppermute x6, waiting for transfers between devices, with_halo(): lax.ppermute(lax.slice_in_dim(block, block.shape[dim] - width, None, axis...  11.9 us
  transfers between devices with their start and end apart: 13, of which 7 were waited for; matrix products, arithmetic and copies ran while one was open for 0% of the time, Pallas kernels for 0%

commit v1 on v0

--- a/solution.py
+++ b/solution.py
@@ -1,3 +1,4 @@
+import functools
 import jax
 import jax.numpy as jnp
 from jax import lax
@@ -8,6 +9,21 @@
 CORIOLIS = 0.5
 GRAVITY = 1.0
 NUDGE = 0.5
+
+
+def test_chunk(x0, where_dim):
+    return jnp.concatenate(
+        jax.lax.all_to_all(
+            jnp.stack([x0 for _ in range(jax.lax.axis_size("particle"))]),
+            axis_name="particle",
+            split_axis=0,
+            concat_axis=0,
+        ),
+        where_dim,
+    )
+
+
+point_resolve = functools.partial(test_chunk, where_dim=0)
 
 
 def with_halo(block, sides, width):
@@ -106,7 +122,7 @@
     state = state * full_mask
     columns = jnp.arange(width_y, dtype=jnp.int32)
     for step in range(STEPS):
-        lines = lax.all_gather(altimetry[step], "particle", axis=0, tiled=True)
+        lines = point_resolve(altimetry[step])
         onehot = (obs_rows[step][:, None] == columns[None, :]).astype(jnp.float32)
         target = jnp.dot(
             lines.T, onehot, precision=lax.Precision.HIGHEST, preferred_element_type=jnp.float32

time: 483 us -> 405 us (0.84)
  blocking collectives: 122 us -> 0 us
  starting transfers between devices: 3.51 us -> 39.3 us
  waiting for transfers between devices: 327 us -> 319 us
  local copies, waits for them, and re-layouts: 0.89 us -> 8.42 us
  other arithmetic: 13.6 us -> 18.8 us
    all_gather x3 -> x0, blocking collectives: 122 us -> none  [per_device(): lines = lax.all_gather(altimetry[step], 'particle', axis=0, tiled=True)]
    all_to_all x0 -> x3, starting transfers between devices: none -> 30.4 us  [test_chunk(): jax.lax.all_to_all(jnp.stack([x0 for _ in range(jax.lax.axis_size('partic...]
    all_gather x1, waiting for transfers between devices: 312 us -> 299 us  [per_device(): piece = lax.all_gather(ensemble, 'particle', axis=0, tiled=True)]
    ppermute x6, starting transfers between devices: 0.5 us -> 7.29 us  [with_halo(): lax.ppermute(lax.slice_in_dim(block, 0, width, axis=dim), axis, backward)]
    unnamed x10 -> x44, local copies, waits for them, and re-layouts: 0.02 us -> 5.1 us
  transfers between devices with their start and end apart: 13 -> 16, of which waited for: 7 -> 9; matrix products, arithmetic and copies ran while one was open for 0% -> 6% of each run, Pallas kernels for 0% -> 0%
where the time goes in v1:
time: 405 us; the launch traced here: 404 us
  waiting for transfers between devices  319 us (79%)
  starting transfers between devices  39.3 us (10%)
  other arithmetic  18.8 us (5%)
  between operations  15.7 us (4%)
  local copies, waits for them, and re-layouts  8.42 us (2%)
    all_gather x1, waiting for transfers between devices, per_device(): piece = lax.all_gather(ensemble, 'particle', axis=0, tiled=True)  299 us
    all_to_all x3, starting transfers between devices, test_chunk(): jax.lax.all_to_all(jnp.stack([x0 for _ in range(jax.lax.axis_size('partic...  30.4 us
    ppermute x6, waiting for transfers between devices, with_halo(): lax.ppermute(lax.slice_in_dim(block, block.shape[dim] - width, None, axis...  15.2 us
  transfers between devices with their start and end apart: 16, of which 9 were waited for; matrix products, arithmetic and copies ran while one was open for 6% of the time, Pallas kernels for 0%

profile of v1, /device:TPU:8, one launch (start us, length us, event | category | flops | bytes accessed | tf_op | source)
XLA Modules:
  0.0 403.9 jit_solution(11025495556610117492)
XLA Ops:
  6.6 0.7 all-gather.2.cloned.1.call-update
  7.3 0.7 reshape.66
  8.0 11.6 %all-to-all-start = ((f32[16,1,128]{2,1,0:T(1,128)}), f32[16,1,128]{2,1,0:T(1,128)S(1)}, u32[]{:S(2)}, u32[]{:S(2)}) async-start(f32[16,1,128]{2,1,0:T(1,128)} %reshape.66), calls=%async_computation | async-start | bytes 16384 | tf_op jit(solution)/shard_map/all_to_all | solution.py:16
  19.6 0.6 dynamic_slice.7
  22.1 0.6 slice_bitcast_fusion.6
  22.9 299.2 %all-gather.2.cloned.1.call-done = f32[16,13,32,1024]{3,2,1,0:T(8,128)} async-done(((f32[1,13,32,1024]{3,2,1,0:T(8,128)}), f32[16,13,32,1024]{3,2,1,0:T(8,128)}) %all-gather.2.cloned.1.call-update) | async-done | bytes 27262992 | tf_op jit(solution)/shard_map/all_gather | solution.py:114
  322.1 1.7 maximum_multiply_fusion
  324.0 0.5 collective-permute-start.1
  324.5 0.6 multiply_bitcast_fusion.1
  325.1 0.7 reshape.64
  325.8 9.2 %all-to-all-start.1 = ((f32[16,1,128]{2,1,0:T(1,128)}), f32[16,1,128]{2,1,0:T(1,128)S(1)}, u32[]{:S(2)}, u32[]{:S(2)}) async-start(f32[16,1,128]{2,1,0:T(1,128)} %reshape.64), calls=%async_computation.1 | async-start | bytes 16384 | tf_op jit(solution)/shard_map/all_to_all | solution.py:16
  335.0 0.5 broadcast.147
  335.5 0.7 reduce.2
  336.3 1.8 multiply_subtract_fusion.2
  338.4 0.3 fusion.3
  338.7 3.4 collective-permute-start.2
  342.2 1.2 collective-permute-done.2
  343.4 3.8 collective-permute-done.3
  347.4 0.6 fusion.54
  348.1 0.7 fusion.80
  348.9 0.5 collective-permute-start.5
  349.4 0.6 broadcast_multiply_fusion.1
  350.0 0.6 stack.11
  350.6 1.4 reshape.62
  352.0 9.6 %all-to-all-start.2 = ((f32[16,1,128]{2,1,0:T(1,128)}), f32[16,1,128]{2,1,0:T(1,128)}, u32[]{:S(2)}, u32[]{:S(2)}) async-start(f32[16,1,128]{2,1,0:T(1,128)} %reshape.62), calls=%async_computation.2 | async-start | bytes 16384 | tf_op jit(solution)/shard_map/all_to_all | solution.py:16
  361.7 0.7 reduce.1
  362.3 0.7 reshape.65
  363.0 1.3 subtract_multiply_fusion.3
  364.3 2.8 multiply_subtract_fusion.1
  367.2 0.5 fusion.32
  367.9 1.2 fusion.7
  369.1 3.1 collective-permute-start.6
  372.3 1.2 collective-permute-done.6
  373.5 3.9 collective-permute-done.7
  377.5 0.4 fusion.41
  378.0 1.2 copy-done
  379.4 0.5 collective-permute-start.9
  379.9 1.4 reduce
  381.4 3.7 collective-permute-done.9
  385.1 0.4 subtract_multiply_fusion.1
  385.5 2.0 multiply_subtract_fusion
  387.6 0.5 fusion.19
  388.1 1.2 fusion.12
  389.3 0.7 collective-permute-start.10
  390.0 1.3 collective-permute-done.10
  391.4 3.8 collective-permute-done.11
  395.3 0.4 fusion.28
  395.7 1.4 maximum_bitcast_fusion
  (75 shorter events, 2.2 us)
Async XLA Ops:
  6.5 0.7 copy-start.12
  6.5 13.0 %copy-start.18 = (s32[16]{0:T(128)S(1)}, s32[16]{0:T(128)}, u32[]{:S(2)}) copy-start(s32[16]{0:T(128)} %param.7) | copy-start | bytes 196
  6.5 15.5 %copy-start.2 = (s32[32,1024]{1,0:T(8,128)S(1)}, s32[32,1024]{1,0:T(8,128)}, u32[]{:S(2)}) copy-start(s32[32,1024]{1,0:T(8,128)} %param.8) | copy-start | bytes 393220
  6.5 15.6 %copy-start.16 = (s32[3,64]{1,0:T(4,128)S(1)}, s32[3,64]{1,0:T(4,128)}, u32[]{:S(2)}) copy-start(s32[3,64]{1,0:T(4,128)} %param.11) | copy-start | bytes 2308
  6.5 315.6 %all-gather.2.cloned.1.call-start = ((), (), s32[]{:S(2)}) async-start(), calls=%async_computation.3 | async-start | bytes 28966912 | tf_op jit(solution)/shard_map/all_gather | solution.py:114
  8.0 317.8 %all-to-all-start = ((f32[16,1,128]{2,1,0:T(1,128)}), f32[16,1,128]{2,1,0:T(1,128)S(1)}, u32[]{:S(2)}, u32[]{:S(2)}) async-start(f32[16,1,128]{2,1,0:T(1,128)} %reshape.66), calls=%async_computation | async-start | bytes 16384 | tf_op jit(solution)/shard_map/all_to_all | solution.py:16
  22.1 316.3 %copy-start.3 = (f32[4,32,1024]{2,1,0:T(8,128)}, f32[4,32,1024]{2,1,0:T(8,128)S(1)}, u32[]{:S(2)}) copy-start(f32[4,32,1024]{2,1,0:T(8,128)S(1)} %fusion.55) | copy-start | bytes 1572868
  22.8 319.3 %copy-start.14 = (s32[64]{0:T(128)}, s32[64]{0:T(128)S(1)}, u32[]{:S(2)}) copy-start(s32[64]{0:T(128)S(1)} %get-tuple-element.49) | copy-start | bytes 772
  322.1 2.4 copy-start.17
  323.9 12.4 %collective-permute-start = (f32[13,1,1024]{2,1,0:T(1,128)S(1)}, f32[13,1,1024]{2,1,0:T(1,128)S(1)}, u32[]{:S(2)}, u32[]{:S(2)}) collective-permute-start(f32[13,1,1024]{2,1,0:T(1,128)S(1)} %get-tuple-element.28), channel_id=1, source_target_pairs={{1,0},{2,1},{3,2},{4,3},{5,4},{6,5},{7,6},{8,7},{9,8},{10,9},{11,1... | collective-permute-start | bytes 159752 | tf_op jit(solution)/shard_map/ppermute | solution.py:38
  324.0 12.3 %collective-permute-start.1 = (f32[13,1,1024]{2,1,0:T(1,128)S(1)}, f32[13,1,1024]{2,1,0:T(1,128)S(1)}, u32[]{:S(2)}, u32[]{:S(2)}) collective-permute-start(f32[13,1,1024]{2,1,0:T(1,128)S(1)} %get-tuple-element.27), channel_id=1, source_target_pairs={{0,1},{1,2},{2,3},{3,4},{4,5},{5,6},{6,7},{7,8},{8,9},{9,10},{10,1... | collective-permute-start | bytes 159752 | tf_op jit(solution)/shard_map/ppermute | solution.py:35
  325.1 13.1 %copy-start.8 = (f32[4]{0:T(128)}, f32[4]{0:T(128)S(1)}, u32[]{:S(2)}) copy-start(f32[4]{0:T(128)S(1)} %get-tuple-element.45) | copy-start | bytes 52
  325.8 26.3 %all-to-all-start.1 = ((f32[16,1,128]{2,1,0:T(1,128)}), f32[16,1,128]{2,1,0:T(1,128)S(1)}, u32[]{:S(2)}, u32[]{:S(2)}) async-start(f32[16,1,128]{2,1,0:T(1,128)} %reshape.64), calls=%async_computation.1 | async-start | bytes 16384 | tf_op jit(solution)/shard_map/all_to_all | solution.py:16
  338.2 9.2 %copy-start.6 = (f32[4]{0:T(128)S(1)}, f32[4]{0:T(128)}, u32[]{:S(2)}) copy-start(f32[4]{0:T(128)} %get-tuple-element.44) | copy-start | bytes 52
  338.2 9.2 %copy-start.10 = (f32[4]{0:T(128)S(1)}, f32[4]{0:T(128)}, u32[]{:S(2)}) copy-start(f32[4]{0:T(128)} %get-tuple-element.46) | copy-start | bytes 52
  338.7 4.7 %collective-permute-start.2 = (f32[1,1,1024]{2,1,0:T(1,128)S(1)}, f32[1,1,1024]{2,1,0:T(1,128)S(1)}, u32[]{:S(2)}, u32[]{:S(2)}) collective-permute-start(f32[1,1,1024]{2,1,0:T(1,128)S(1)} %get-tuple-element.39), channel_id=1, source_target_pairs={{1,0},{2,1},{3,2},{4,3},{5,4},{6,5},{7,6},{8,7},{9,8},{10,9},{11,1... | collective-permute-start | bytes 12296 | tf_op jit(solution)/shard_map/ppermute | solution.py:38
  342.1 5.1 %collective-permute-start.3 = (f32[1,1,1024]{2,1,0:T(1,128)S(1)}, f32[1,1,1024]{2,1,0:T(1,128)S(1)}, u32[]{:S(2)}, u32[]{:S(2)}) collective-permute-start(f32[1,1,1024]{2,1,0:T(1,128)S(1)} %get-tuple-element.40), channel_id=1, source_target_pairs={{0,1},{1,2},{2,3},{3,4},{4,5},{5,6},{6,7},{7,8},{8,9},{9,10},{10,1... | collective-permute-start | bytes 12296 | tf_op jit(solution)/shard_map/ppermute | solution.py:35
  348.9 14.1 %collective-permute-start.4 = (f32[13,1,1024]{2,1,0:T(1,128)}, f32[13,1,1024]{2,1,0:T(1,128)}, u32[]{:S(2)}, u32[]{:S(2)}) collective-permute-start(f32[13,1,1024]{2,1,0:T(1,128)} %get-tuple-element.25), channel_id=1, source_target_pairs={{1,0},{2,1},{3,2},{4,3},{5,4},{6,5},{7,6},{8,7},{9,8},{10,9},{11,1... | collective-permute-start | bytes 159752 | tf_op jit(solution)/shard_map/ppermute | solution.py:38
  348.9 14.1 %collective-permute-start.5 = (f32[13,1,1024]{2,1,0:T(1,128)}, f32[13,1,1024]{2,1,0:T(1,128)}, u32[]{:S(2)}, u32[]{:S(2)}) collective-permute-start(f32[13,1,1024]{2,1,0:T(1,128)} %get-tuple-element.24), channel_id=1, source_target_pairs={{0,1},{1,2},{2,3},{3,4},{4,5},{5,6},{6,7},{7,8},{8,9},{9,10},{10,1... | collective-permute-start | bytes 159752 | tf_op jit(solution)/shard_map/ppermute | solution.py:35
  352.0 27.8 %all-to-all-start.2 = ((f32[16,1,128]{2,1,0:T(1,128)}), f32[16,1,128]{2,1,0:T(1,128)}, u32[]{:S(2)}, u32[]{:S(2)}) async-start(f32[16,1,128]{2,1,0:T(1,128)} %reshape.62), calls=%async_computation.2 | async-start | bytes 16384 | tf_op jit(solution)/shard_map/all_to_all | solution.py:16
  364.3 2.9 copy-start.9
  364.3 2.9 copy-start.11
  367.1 0.8 copy-start.4
  367.1 0.8 copy-start.5
  367.2 0.7 copy-start.15
  367.2 5.0 %copy-start.13 = (s32[64]{0:T(128)S(1)}, s32[64]{0:T(128)}, u32[]{:S(2)}) copy-start(s32[64]{0:T(128)} %get-tuple-element.48) | copy-start | bytes 772
  367.2 10.3 %copy-start.7 = (f32[4]{0:T(128)S(1)}, f32[4]{0:T(128)}, u32[]{:S(2)}) copy-start(f32[4]{0:T(128)} %get-tuple-element.44) | copy-start | bytes 52
  369.1 4.4 %collective-permute-start.6 = (f32[1,1,1024]{2,1,0:T(1,128)S(1)}, f32[1,1,1024]{2,1,0:T(1,128)S(1)}, u32[]{:S(2)}, u32[]{:S(2)}) collective-permute-start(f32[1,1,1024]{2,1,0:T(1,128)S(1)} %get-tuple-element.35), channel_id=1, source_target_pairs={{1,0},{2,1},{3,2},{4,3},{5,4},{6,5},{7,6},{8,7},{9,8},{10,9},{11,1... | collective-permute-start | bytes 12296 | tf_op jit(solution)/shard_map/ppermute | solution.py:38
  372.2 5.2 %collective-permute-start.7 = (f32[1,1,1024]{2,1,0:T(1,128)S(1)}, f32[1,1,1024]{2,1,0:T(1,128)S(1)}, u32[]{:S(2)}, u32[]{:S(2)}) collective-permute-start(f32[1,1,1024]{2,1,0:T(1,128)S(1)} %get-tuple-element.36), channel_id=1, source_target_pairs={{0,1},{1,2},{2,3},{3,4},{4,5},{5,6},{6,7},{7,8},{8,9},{9,10},{10,1... | collective-permute-start | bytes 12296 | tf_op jit(solution)/shard_map/ppermute | solution.py:35
  378.0 1.2 copy-start
  379.3 2.1 collective-permute-start.8
  379.4 5.7 %collective-permute-start.9 = (f32[13,1,1024]{2,1,0:T(1,128)S(1)}, f32[13,1,1024]{2,1,0:T(1,128)S(1)}, u32[]{:S(2)}, u32[]{:S(2)}) collective-permute-start(f32[13,1,1024]{2,1,0:T(1,128)S(1)} %get-tuple-element.20), channel_id=1, source_target_pairs={{0,1},{1,2},{2,3},{3,4},{4,5},{5,6},{6,7},{7,8},{8,9},{9,10},{10,1... | collective-permute-start | bytes 159752 | tf_op jit(solution)/shard_map/ppermute | solution.py:35
  381.3 4.2 %copy-start.1 = (f32[13,32,1024]{2,1,0:T(8,128)S(1)}, f32[13,32,1024]{2,1,0:T(8,128)}, u32[]{:S(2)}) copy-start(f32[13,32,1024]{2,1,0:T(8,128)} %copy-done) | copy-start | bytes 5111812
  389.3 2.0 collective-permute-start.10
  390.0 5.1 %collective-permute-start.11 = (f32[1,1,1024]{2,1,0:T(1,128)S(1)}, f32[1,1,1024]{2,1,0:T(1,128)S(1)}, u32[]{:S(2)}, u32[]{:S(2)}) collective-permute-start(f32[1,1,1024]{2,1,0:T(1,128)S(1)} %get-tuple-element.32), channel_id=1, source_target_pairs={{0,1},{1,2},{2,3},{3,4},{4,5},{5,6},{6,7},{7,8},{8,9},{9,10},{10,1... | collective-permute-start | bytes 12296 | tf_op jit(solution)/shard_map/ppermute | solution.py:35
Sparse Core Ops, SparseCore 0:
  9.8 312.2 all-gather.1
